TPU v7x, 256 devices: a whole 4x4x8 slice. The times are simulated.
256 devices in a mesh: band: 4 (over y), pw: 64 (over z, x, core).
Axes of the slice: x: 4, y: 4, z: 8, core: 2. Of those that a mesh axis runs over, the one named last changes fastest.
Arguments:
- coefficients: bfloat16 [2, 64, 655360], P(None, 'band', 'pw'), may hold values from -0.0078125 to 0.0078125
- miller: int32 [3, 655360], P(None, 'pw'), may hold values from -66 to 66, as said below
- column_count: int32 [64], P('pw'), may hold values from 3413 to 10240, as said below
- positions: int32 [3, 128], replicated, may hold values from 0 to 4095
- species: int32 [128], replicated, may hold values from 0 to 1
- atom_slot: int32 [128], replicated, may hold values from 0 to 127, each once
- radius: float32 [2, 8], replicated, as said below
- strength: float32 [2, 8], replicated, as said below
- occupation: int32 [64], P('band'), may hold values from 0 to 4
Outputs:
- atom_stress: float32 [6, 128], P(None, 'pw')
- kinetic_stress: float32 [6], replicated
Inputs may be any that keep to these rules, and one draw needn't show every extreme that they name: `column_count`: each shard's live columns come first; its remaining slots up to 10240 are padding whose coefficients and Miller indices are ignored. Some shard is full. `miller`: every column's indices lie in this range, padding too. `radius`: radii lie between 0.2 and 3.2. `strength`: strengths lie between -1 and 1.
All inputs are finite; a program needn't handle non-finite values.
Results may differ from a plain program's by a relative error of at most 0.0044.
Values sent between devices are 32-bit elements; how exact they have to be, the bound alone decides.
A program may use at most 64 MiB of HBM per device.

v0:
```python
import math

import jax
import jax.numpy as jnp
from jax import lax
from jax.sharding import PartitionSpec as P

BANDS = 64
POS_GRID = 4096


recip_unit = 0.125
full_turn = 2.0 * math.pi
diagonal_flags = (1.0, 1.0, 1.0, 0.0, 0.0, 0.0)


def strain_weights(wave_vec):
    comp_x = wave_vec[0]
    comp_y = wave_vec[1]
    comp_z = wave_vec[2]
    return jnp.stack(
        [
            jnp.ones_like(comp_x),
            comp_x * comp_x,
            comp_y * comp_y,
            comp_z * comp_z,
            comp_y * comp_z,
            comp_z * comp_x,
            comp_x * comp_y,
        ]
    )


def species_table(table_in, kinds_of):
    kind_index = jnp.arange(table_in.shape[0], dtype=jnp.int32)
    picked = kinds_of[:, None, None] == kind_index[None, :, None]
    return jnp.sum(jnp.where(picked, table_in[None], 0.0), axis=1)


def on_device(
    coefficients, miller, column_count, positions, species, atom_slot, radius, strength, occupation
):
    band_dev = coefficients.shape[1]
    columns = coefficients.shape[2]
    block_len = math.gcd(512, columns)
    atom_total = species.shape[0]
    per_atom = radius.shape[1]
    live_count = column_count[0]
    slot_match = atom_slot[:, None] == jnp.arange(atom_total, dtype=jnp.int32)[None, :]
    slot_places = jnp.sum(jnp.where(slot_match[None], positions[:, :, None], 0), axis=1)
    slot_kinds = jnp.sum(jnp.where(slot_match, species[:, None], 0), axis=0)
    radius_sq = species_table(radius, slot_kinds) ** 2
    potency = species_table(strength, slot_kinds)
    filling = occupation.astype(jnp.float32) * 0.5
    live_mask = jnp.arange(columns, dtype=jnp.int32) < live_count
    all_weights = strain_weights(recip_unit * miller.astype(jnp.float32))
    widened = coefficients.astype(jnp.float32)
    density = jnp.sum(filling[None, :, None] * widened * widened, axis=(0, 1))
    kinetic = (
        0.5 / BANDS * jnp.sum(all_weights[1:] * jnp.where(live_mask, density, 0.0)[None], axis=1)
    )
    owned_atoms = atom_total // lax.axis_size("pw")
    rows_owned = owned_atoms * per_atom
    row_count = atom_total * per_atom

    def add_block(block_index, running):
        anchor = block_index * block_len
        indices = lax.dynamic_slice_in_dim(miller, anchor, block_len, 1)
        coef_block = lax.dynamic_slice_in_dim(coefficients, anchor, block_len, 2)
        wave_vec = recip_unit * indices.astype(jnp.float32)
        wave_sq = jnp.sum(wave_vec * wave_vec, axis=0)
        is_live = anchor + jnp.arange(block_len, dtype=jnp.int32) < live_count
        masked = jnp.where(is_live, coef_block.astype(jnp.float32), 0.0)
        weighted = (
            (strain_weights(wave_vec)[:, None, None, :] * masked[None])
            .astype(jnp.bfloat16)
            .reshape(-1, block_len)
        )
        grid_turns = jnp.mod(
            jnp.sum(indices[:, :, None] * slot_places[:, None, :], axis=0), POS_GRID
        )
        phase_angle = grid_turns.astype(jnp.float32) * (full_turn / POS_GRID)
        radial = jnp.exp(-0.5 * radius_sq[None] * wave_sq[:, None, None])
        cosine = (radial * jnp.cos(phase_angle)[:, :, None]).reshape(block_len, -1)
        sine_part = (radial * jnp.sin(phase_angle)[:, :, None]).reshape(block_len, -1)
        paired = jnp.concatenate([cosine, sine_part], axis=1).astype(jnp.bfloat16)
        return running + lax.dot_general(
            paired, weighted, (((0,), (1,)), ((), ())), preferred_element_type=jnp.float32
        )

    blocks_live = (live_count + block_len - 1) // block_len
    summed = lax.fori_loop(
        0, blocks_live, add_block, jnp.zeros((2 * row_count, 14 * band_dev), jnp.float32)
    )
    summed = summed.reshape(2, row_count, 7, 2, band_dev)
    real_part = summed[0, :, :, 0] - summed[1, :, :, 1]
    imag_part = summed[0, :, :, 1] + summed[1, :, :, 0]
    every_row, kinetic_cols = lax.psum((jnp.stack([real_part, imag_part], axis=2), kinetic), "pw")
    owned_rows = lax.dynamic_slice_in_dim(
        every_row, lax.axis_index("pw") * rows_owned, rows_owned, 0
    )
    atom_first = lax.axis_index("pw") * owned_atoms
    spread_own = lax.dynamic_slice_in_dim(radius_sq, atom_first, owned_atoms, 0).reshape(-1)
    potency_own = lax.dynamic_slice_in_dim(potency, atom_first, owned_atoms, 0).reshape(-1)
    diag_flags = jnp.array(diagonal_flags, jnp.float32)
    base_re = owned_rows[:, 0, 0]
    base_im = owned_rows[:, 0, 1]
    strain_re = (
        spread_own[:, None, None] * owned_rows[:, 1:, 0]
        - 0.5 * diag_flags[None, :, None] * base_re[:, None]
    )
    strain_im = (
        spread_own[:, None, None] * owned_rows[:, 1:, 1]
        - 0.5 * diag_flags[None, :, None] * base_im[:, None]
    )
    band_part = jnp.sum(
        filling[None, None, :] * (base_re[:, None] * strain_re + base_im[:, None] * strain_im),
        axis=2,
    )
    band_part = (2.0 * potency_own[:, None] * band_part).reshape(-1, per_atom, 6).sum(axis=1).T
    atom_stress, kinetic_stress = lax.psum((band_part, kinetic_cols), "band")
    return (atom_stress, kinetic_stress)


def solution(mesh):
    in_specs = (P(None, "band", "pw"), P(None, "pw"), P("pw"), P(), P(), P(), P(), P(), P("band"))
    out_specs = (P(None, "pw"), P())
    return jax.shard_map(
        on_device, mesh=mesh, in_specs=in_specs, out_specs=out_specs, check_vma=False
    )
```

profile of v0, /device:TPU:1, one launch (start us, length us, event | category | flops | bytes accessed | tf_op | source)
XLA Modules:
  0.0 306.1 jit_solution(14176744318651528149)
XLA Ops:
  11.4 83.1 %while.12 = (s32[]{:T(128)}, f32[2048,224]{0,1:T(8,128)S(1)}, s32[]{:T(128)}, f32[128,8]{1,0:T(8,128)S(1)}, s32[3,10240]{1,0:T(4,128)S(1)}, /*index=5*/s32[3,128...) while((s32[]{:T(128)}, f32[2048,224]{0,1:T(8,128)S(1)}, ...), condition=%wide.region_7.8_spmd, body=%wide.region_4.7_spmd.sunk | while | flops 478492160 | bytes 13851363 | solution.py:92
  12.7 1.1 fusion.23
  16.8 1.1 fusion.23
  29.3 1.1 fusion.23
  33.5 1.1 fusion.23
  37.6 1.1 fusion.23
  41.8 1.1 fusion.23
  54.2 1.1 fusion.23
  58.4 1.1 fusion.23
  62.5 1.1 fusion.23
  66.7 1.1 fusion.23
  70.8 1.1 fusion.23
  79.2 1.1 fusion.23
  83.3 1.1 fusion.23
  87.5 1.1 fusion.23
  91.6 1.1 fusion.23
  94.6 2.8 reshape.174
  97.4 2.2 fusion.12
  99.5 2.2 fusion.14
  101.7 1.8 pad_maximum_fusion
  104.7 123.9 %psum.30 = f32[6]{0:T(128)S(1)} all-reduce(f32[6]{0:T(128)S(1)} %broadcast_multiply_fusion.1), channel_id=1, replica_groups=mesh['band'=4,'pw'=64] {'pw'}, use_global_device_ids=true, to_apply=%region_14.15 | all-reduce | flops 6 | bytes 48 | tf_op jit(solution)/shard_map/psum | solution.py:98
  228.9 58.2 %all-reduce.3.cloned.1.call-done = f32[1024,7,2,16]{0,2,3,1:T(2,128)} async-done(((f32[1024,7,2,16]{0,2,3,1:T(2,128)}), f32[1024,7,2,16]{0,2,3,1:T(2,128)}) %all-reduce.3.cloned.1.call-update) | async-done | bytes 917520 | tf_op jit(solution)/shard_map/psum | solution.py:98
  288.1 1.2 constant_dynamic-slice_fusion.5
  289.6 9.0 %all-reduce = (f32[6,2]{1,0:T(8,128)S(1)}, f32[6]{0:T(128)}) all-reduce(f32[6,2]{1,0:T(8,128)S(1)} %bitcast.49, f32[6]{0:T(128)S(1)} %psum.30), channel_id=1, replica_groups=mesh['band'=4,'pw'=64] {'band'}, use_global_device_ids=true, to_apply=%region_11.12 | all-reduce | flops 18 | bytes 144 | tf_op jit(solution)/shard_map/psum | solution.py:121
  (380 shorter events, 71.4 us)
Async XLA Ops:
  7.2 4.3 %copy-start.2 = (s32[3,10240]{1,0:T(4,128)S(1)}, s32[3,10240]{1,0:T(4,128)}, u32[]{:S(2)}) copy-start(s32[3,10240]{1,0:T(4,128)} %param.13) | copy-start | bytes 368644
  7.2 4.3 %copy-start = (bf16[2,16,10240]{2,1,0:T(8,128)(2,1)S(1)}, bf16[2,16,10240]{2,1,0:T(8,128)(2,1)}, u32[]{:S(2)}) copy-start(bf16[2,16,10240]{2,1,0:T(8,128)(2,1)} %param.12) | copy-start | bytes 1966084
  7.2 280.0 %all-reduce.3.cloned.1.call-start = ((), (), s32[]{:S(2)}) async-start(), calls=%async_computation | async-start | bytes 1835008 | tf_op jit(solution)/shard_map/psum | solution.py:98
  14.5 1.1 copy-start.1
  18.7 1.1 copy-start.1
  22.8 1.1 copy-start.1
  27.0 1.1 copy-start.1
  31.1 1.1 copy-start.1
  35.3 1.1 copy-start.1
  39.5 1.1 copy-start.1
  43.6 1.1 copy-start.1
  47.8 1.1 copy-start.1
  51.9 1.1 copy-start.1
  56.1 1.1 copy-start.1
  60.2 1.1 copy-start.1
  64.4 1.1 copy-start.1
  68.5 1.1 copy-start.1
  72.7 1.1 copy-start.1
  76.9 1.1 copy-start.1
  81.0 1.1 copy-start.1
  85.2 1.1 copy-start.1
  89.3 1.1 copy-start.1
  101.7 1.9 copy-start.4
  103.5 185.8 %copy-start.3 = (f32[6]{0:T(128)S(1)}, f32[6]{0:T(128)}, u32[]{:S(2)}) copy-start(f32[6]{0:T(128)} %constant.112) | copy-start | bytes 76
  (1 other events, 1.1 us)
Sparse Core Ops, SparseCore 0:
  103.6 183.4 all-reduce.2
where the time goes:
time: 311 us; the launch traced here: 306 us
  blocking collectives  133 us (43%)
  other arithmetic  61.8 us (20%)
  waiting for transfers between devices  58.3 us (19%)
  local copies, waits for them, and re-layouts  18.2 us (6%)
  matrix products  17.7 us (6%)
  between operations  14.9 us (5%)
    psum x1, blocking collectives, on_device(): lax.psum((jnp.stack([real_part, imag_part], axis=2), kinetic), 'pw')  124 us
    psum x1, waiting for transfers between devices, on_device(): lax.psum((jnp.stack([real_part, imag_part], axis=2), kinetic), 'pw')  58.2 us
    cos x20, other arithmetic, add_block(): cosine = (radial * jnp.cos(phase_angle)[:, :, None]).reshape(block_len, -1)  21.6 us
    dot_general x20, matrix products, add_block(): lax.dot_general(paired, weighted, (((0,), (1,)), ((), ())), preferred_ele...  17.7 us
    lt x20, other arithmetic, add_block(): is_live = anchor + jnp.arange(block_len, dtype=jnp.int32) < live_count  13 us
    another operation x20, other arithmetic  9.74 us
    psum x1, blocking collectives, on_device(): atom_stress, kinetic_stress = lax.psum((band_part, kinetic_cols), 'band')  9.04 us
  transfers between devices with their start and end apart: 1, of which 1 were waited for; matrix products, arithmetic and copies ran while one was open for 0% of the time, Pallas kernels for 0%

commit v1 on v0

v1 whole, which is shorter than its diff:
```python
import functools
import math

import jax
import jax.numpy as jnp
from jax import lax
from jax.experimental import pallas as pl
from jax.experimental.pallas import tpu as pltpu
from jax.sharding import PartitionSpec as P

BANDS = 64
BLOCK = 512
SIN_POLY = (4.44287957, -7.30781668, 3.59777418, -0.79119939)
COS_POLY = (1.41420401, -6.97763732, 5.71518787, -1.72821389)
ROUNDER = 12582912.0
F32 = jnp.float32
BF16 = jnp.bfloat16
NT = (((1,), (1,)), ((), ()))
NN = (((1,), (0,)), ((), ()))


def poly(coefs, y):
    total = coefs[-1]
    for value in coefs[-2::-1]:
        total = total * y + value
    return total


def split(x):
    high = x.astype(BF16)
    return high, (x - high.astype(F32)).astype(BF16)


def iota(shape, axis):
    return lax.broadcasted_iota(jnp.int32, shape, axis)


def kernel(
    n_pw, n_band, coef_ref, miller_ref, count_ref, pos_ref, species_ref, slot_ref, radius_ref, strength_ref,
    occ_ref, stress_ref, kin_ref,
    e_ref, u_ref, w_ref, acc_ref, kacc_ref, out_ref, bt_ref, zbuf, zrecv, own, gath, fbuf, frecv, bsend, brecv,
    sig_ref, send_sem, recv_sem,
):
    columns = coef_ref.shape[2]
    bands = coef_ref.shape[1]
    me = lax.axis_index("pw")
    me_band = lax.axis_index("band")
    steps = columns // BLOCK
    atoms = 128

    barrier = pltpu.get_barrier_semaphore()

    def greet(d, carry):
        pl.semaphore_signal(barrier, inc=1, device_id={"pw": lax.rem(me + d, n_pw)})
        return carry

    lax.fori_loop(1, n_pw, greet, 0)
    for d in range(1, n_band):
        pl.semaphore_signal(barrier, inc=1, device_id={"band": lax.rem(me_band + d, n_band)})

    one_hot = slot_ref[...] == iota((atoms, atoms), 0)
    pos = pos_ref[...]
    parts = [pos & ~63, pos & 63]
    place_rows = []
    for part, order in zip(parts, ((0, 1, 2), (1, 2, 0))):
        for i in order:
            row = part[i : i + 1, :].astype(F32)
            place_rows.append(jnp.sum(jnp.where(one_hot, row, 0.0), axis=1, keepdims=True) * (1.0 / 4096.0))
    place_rows += [jnp.zeros((atoms, 1), F32)] * 2
    places = jnp.zeros((atoms, 8), F32)
    lane8 = iota((atoms, 8), 1)
    for i in range(6):
        places = jnp.where(lane8 == i, place_rows[i], places)
    places = places.astype(BF16)
    kind = jnp.sum(jnp.where(one_hot, species_ref[...].astype(F32), 0.0), axis=1, keepdims=True)

    row8 = iota((8, 1), 0)
    decay = []
    for s in range(2):
        column = jnp.zeros((8, 1), F32)
        for p in range(8):
            r = radius_ref[s, p]
            column = jnp.where(row8 == p, -0.5 * r * r, column)
        decay.append(column)
    row_n = iota((bands, 1), 0)
    filling = jnp.zeros((bands, 1), F32)
    for n in range(bands):
        filling = jnp.where(row_n == n, occ_ref[0, n].astype(F32) * 0.5, filling)

    acc_ref[...] = jnp.zeros_like(acc_ref)
    kacc_ref[...] = jnp.zeros_like(kacc_ref)
    count = count_ref[0]

    def build(step, carry):
        base = pl.multiple_of(step * BLOCK, BLOCK)
        cols = pl.ds(base, BLOCK)
        index = miller_ref[:, cols].astype(F32)
        x, y, z = (index[i : i + 1] for i in range(3))
        zero = jnp.zeros((2, BLOCK), F32)
        index8 = jnp.concatenate([x, y, z, y, z, x, zero], axis=0)
        turns = lax.dot_general(places, index8.astype(BF16), NN, preferred_element_type=F32)
        r = turns - jnp.round(turns)
        rr = r * r
        sine_half = poly(SIN_POLY, rr) * r
        cosine_half = poly(COS_POLY, rr)
        cosine = 1.0 - sine_half * sine_half
        sine = sine_half * cosine_half
        for half, value in enumerate((cosine, sine)):
            high, low = split(value)
            e_ref[0, half * atoms : (half + 1) * atoms, cols] = high
            e_ref[1, half * atoms : (half + 1) * atoms, cols] = low
        weights = index8 * jnp.concatenate([x, y, z, z, x, y, zero], axis=0) * (1.0 / 64.0)
        wave_sq = weights[0:1] + weights[1:2] + weights[2:3]
        high, low = split(weights)
        w_ref[:, cols] = jnp.concatenate([high.astype(F32), low.astype(F32)], axis=0).astype(BF16)
        live = (iota((1, BLOCK), 1) + base) < count
        coef = [coef_ref[ri, :, cols].astype(F32) for ri in range(2)]
        for s in range(2):
            radial = jnp.where(live, jnp.exp(decay[s] * wave_sq), 0.0)
            for p in range(8):
                row = radial[p : p + 1]
                for ri in range(2):
                    u_ref[pl.ds((s * 2 + ri) * atoms + p * bands, bands), cols] = (row * coef[ri]).astype(BF16)
        density = jnp.sum(filling * (coef[0] * coef[0] + coef[1] * coef[1]), axis=0, keepdims=True)
        moment = weights * jnp.where(live, density, 0.0)
        kacc_ref[...] += sum(moment[:, 128 * i : 128 * (i + 1)] for i in range(BLOCK // 128))
        u = u_ref[:, cols]
        acc_ref[...] += lax.dot_general(
            e_ref[0, :, cols], u, NT, preferred_element_type=F32
        ) + lax.dot_general(e_ref[1, :, cols], u, NT, preferred_element_type=F32)
        return carry

    lax.fori_loop(0, steps, build, 0)

    rows_each = 256 // n_pw
    cross = [[], []]
    for s in range(2):
        re, im = (slice((2 * s + ri) * 128, (2 * s + ri + 1) * 128) for ri in range(2))
        cross[0].append(acc_ref[0:128, re] - acc_ref[128:256, im])
        cross[1].append(acc_ref[0:128, im] + acc_ref[128:256, re])
    for ri in range(2):
        mixed = jnp.where(kind == 0.0, cross[ri][0], cross[ri][1])
        for i in range(n_pw // 2):
            zbuf[ri * (n_pw // 2) + i] = mixed[i * rows_each : (i + 1) * rows_each]

    pl.semaphore_wait(barrier, n_pw - 1 + n_band - 1)

    def scatter(source, landing, phase):
        def send(d, carry):
            to = lax.rem(me + d, n_pw)
            pltpu.make_async_remote_copy(
                src_ref=source(to), dst_ref=landing.at[me], send_sem=send_sem.at[phase], recv_sem=recv_sem.at[phase],
                device_id={"pw": to},
            ).start()
            return carry

        lax.fori_loop(1, n_pw, send, 0)

    def settle(buf, phase, count):
        block = buf.at[pl.ds(0, count)]
        pltpu.make_async_copy(block, block, recv_sem.at[phase]).wait()
        pltpu.make_async_copy(block, block, send_sem.at[phase]).wait()

    scatter(lambda to: zbuf.at[to], zrecv, 0)
    zrecv[me] = zbuf[me]
    settle(zrecv, 0, n_pw - 1)
    own[...] = jnp.sum(zrecv[...], axis=0)
    scatter(lambda to: own, gath, 1)
    gath[me] = own[...]

    lane = iota((1, 128), 1)
    band_lane = lax.rem(lane, bands)
    proj_lane = lane // bands
    fill_lane = jnp.zeros((1, 128), F32)
    for n in range(bands):
        fill_lane = jnp.where(band_lane == n, occ_ref[0, n].astype(F32) * 0.5, fill_lane)
    plain, spread = [], []
    for s in range(2):
        a = jnp.zeros((1, 128), F32)
        b = jnp.zeros((1, 128), F32)
        for p in range(8):
            r = radius_ref[s, p]
            a = jnp.where(proj_lane == p, strength_ref[s, p], a)
            b = jnp.where(proj_lane == p, 2.0 * strength_ref[s, p] * (r * r), b)
        plain.append(a * fill_lane)
        spread.append(b * fill_lane)
    settle(gath, 1, n_pw - 1)
    total = [
        jnp.concatenate([gath[ri * (n_pw // 2) + i] for i in range(n_pw // 2)], axis=0) for ri in range(2)
    ]
    norm = total[0] * total[0] + total[1] * total[1]
    norm = jnp.sum(norm * jnp.where(kind == 0.0, plain[0], plain[1]), axis=1, keepdims=True) * (1.0 / n_pw)
    for s in range(2):
        scale = jnp.where(kind == float(s), spread[s], 0.0)
        back_re, back_im = total[0] * scale, total[1] * scale
        for ri, pair in enumerate(((back_re, back_im), (back_im, -back_re))):
            lanes = slice((2 * s + ri) * 128, (2 * s + ri + 1) * 128)
            for half in range(2):
                high, low = split(pair[0] if half == 0 else pair[1])
                bt_ref[half * 128 : (half + 1) * 128, lanes] = high
                bt_ref[256 + half * 128 : 256 + (half + 1) * 128, lanes] = low
    out_ref[...] = jnp.zeros_like(out_ref)

    def contract(step, carry):
        base = pl.multiple_of(step * BLOCK, BLOCK)
        cols = pl.ds(base, BLOCK)
        u = u_ref[:, cols]
        back = lax.dot_general(bt_ref[0:256], u, NN, preferred_element_type=F32) + lax.dot_general(
            bt_ref[256:512], u, NN, preferred_element_type=F32
        )
        value = [e_ref[0, h * 128 : (h + 1) * 128, cols].astype(F32) for h in range(2)]
        low = [e_ref[1, h * 128 : (h + 1) * 128, cols].astype(F32) for h in range(2)]
        both = back[0:128] * (value[0] + low[0]) + back[128:256] * (value[1] + low[1])
        high, low = split(both)
        w = w_ref[:, cols]
        out_ref[...] += lax.dot_general(high, w, NT, preferred_element_type=F32) + lax.dot_general(
            low, w, NT, preferred_element_type=F32
        )
        return carry

    lax.fori_loop(0, steps, contract, 0)

    kin = jnp.sum(kacc_ref[...], axis=1, keepdims=True) * (0.5 / BANDS)
    kin_row = jnp.sum(jnp.where(iota((8, 128), 1) == iota((8, 128), 0) + 8, kin, 0.0), axis=0, keepdims=True)
    stress = out_ref[:, 0:8] + out_ref[:, 8:16] - jnp.where(iota((1, 8), 1) < 3, norm, 0.0)
    sig_ref[...] = jnp.broadcast_to(kin_row, sig_ref.shape)
    sig_ref[:, 0:8] = stress
    per = atoms // n_pw
    for i in range(n_pw):
        fbuf[i] = sig_ref[i * per : (i + 1) * per]
    scatter(lambda to: fbuf.at[to], frecv, 2)
    frecv[me] = fbuf[me]
    settle(frecv, 2, n_pw - 1)
    bsend[...] = jnp.sum(frecv[...], axis=0)
    for d in range(1, n_band):
        pltpu.make_async_remote_copy(
            src_ref=bsend, dst_ref=brecv.at[me_band], send_sem=send_sem.at[3], recv_sem=recv_sem.at[3],
            device_id={"band": lax.rem(me_band + d, n_band)},
        ).start()
    brecv[me_band] = bsend[...]
    settle(brecv, 3, n_band - 1)
    final = jnp.sum(brecv[...], axis=0)
    kin_ref[...] = final[0:1, 8:14]
    stress_ref[...] = final[:, 0:6]


def solution(mesh):
    n_pw, n_band = mesh.shape["pw"], mesh.shape["band"]

    def on_device(
        coefficients, miller, column_count, positions, species, atom_slot, radius, strength, occupation
    ):
        columns = coefficients.shape[2]
        vmem = pl.BlockSpec(memory_space=pltpu.VMEM)
        smem = pl.BlockSpec(memory_space=pltpu.SMEM)
        per = 128 // n_pw
        rows = 256 // n_pw
        stress, kinetic = pl.pallas_call(
            functools.partial(kernel, n_pw, n_band),
            out_shape=(jax.ShapeDtypeStruct((per, 6), F32), jax.ShapeDtypeStruct((1, 6), F32)),
            in_specs=[vmem, vmem, smem, vmem, vmem, vmem, smem, smem, smem],
            out_specs=(vmem, vmem),
            scratch_shapes=[
                pltpu.VMEM((2, 256, columns), BF16),
                pltpu.VMEM((512, columns), BF16),
                pltpu.VMEM((16, columns), BF16),
                pltpu.VMEM((256, 512), F32),
                pltpu.VMEM((8, 128), F32),
                pltpu.VMEM((128, 16), F32),
                pltpu.VMEM((512, 512), BF16),
                pltpu.VMEM((n_pw, rows, 128), F32),
                pltpu.VMEM((n_pw, rows, 128), F32),
                pltpu.VMEM((rows, 128), F32),
                pltpu.VMEM((n_pw, rows, 128), F32),
                pltpu.VMEM((n_pw, per, 128), F32),
                pltpu.VMEM((n_pw, per, 128), F32),
                pltpu.VMEM((per, 128), F32),
                pltpu.VMEM((n_band, per, 128), F32),
                pltpu.VMEM((128, 128), F32),
                pltpu.SemaphoreType.DMA((4,)),
                pltpu.SemaphoreType.DMA((4,)),
            ],
            compiler_params=pltpu.CompilerParams(
                collective_id=0, has_side_effects=True, vmem_limit_bytes=60 * 1024 * 1024
            ),
        )(
            coefficients, miller, column_count, positions, species[None], atom_slot[None], radius, strength,
            occupation[None],
        )
        return stress.T, kinetic.reshape(6)

    in_specs = (P(None, "band", "pw"), P(None, "pw"), P("pw"), P(), P(), P(), P(), P(), P("band"))
    return jax.shard_map(
        on_device, mesh=mesh, in_specs=in_specs, out_specs=(P(None, "pw"), P()), check_vma=False
    )
```

time: 311 us -> 66.6 us (0.21); the launches traced: 306 us -> 66.4 us
  blocking collectives: 133 us -> 0 us
  Pallas kernels: 0 us -> 63.3 us
  other arithmetic: 61.8 us -> 0 us
  waiting for transfers between devices: 58.3 us -> 0 us
  matrix products: 17.7 us -> 0 us
  local copies, waits for them, and re-layouts: 18.2 us -> 1.8 us
  between operations: 14.9 us -> 1.3 us
    psum x2 -> x0, blocking collectives: 133 us -> none  [the longest x1 124 us: on_device(): lax.psum((jnp.stack([real_part, imag_part], axis=2), kinetic), 'pw')]
    pallas_call x0 -> x1, Pallas kernels: none -> 63.3 us  [on_device(): pl.pallas_call(functools.partial(kernel, n_pw, n_band), out_shape=(jax.Sh...]
    psum x1 -> x0, waiting for transfers between devices: 58.2 us -> none  [on_device(): lax.psum((jnp.stack([real_part, imag_part], axis=2), kinetic), 'pw')]
    cos x20 -> x0, other arithmetic: 21.6 us -> none  [add_block(): cosine = (radial * jnp.cos(phase_angle)[:, :, None]).reshape(block_len, -1)]
    dot_general x20 -> x0, matrix products: 17.7 us -> none  [add_block(): lax.dot_general(paired, weighted, (((0,), (1,)), ((), ())), preferred_ele...]
    lt x20 -> x0, other arithmetic: 13 us -> none  [add_block(): is_live = anchor + jnp.arange(block_len, dtype=jnp.int32) < live_count]
    another operation x21 -> x0, other arithmetic: 11.5 us -> none
    reduce_sum x47 -> x0, other arithmetic: 8.97 us -> none  [the longest x20 5.31 us: add_block(): jnp.sum(indices[:, :, None] * slot_places[:, None, :], axis=0)]
  transfers between devices with their start and end apart: 1 -> 0, of which waited for: 1 -> 0; matrix products, arithmetic and copies ran while one was open for 0% -> 0% of each run, Pallas kernels for 0% -> 0%
where the time goes in v1:
time: 66.6 us; the launch traced here: 66.4 us
  Pallas kernels  63.3 us (95%)
  local copies, waits for them, and re-layouts  1.8 us (3%)
  between operations  1.3 us (2%)
    pallas_call x1, Pallas kernels, on_device(): pl.pallas_call(functools.partial(kernel, n_pw, n_band), out_shape=(jax.Sh...  63.3 us
    unnamed x6, local copies, waits for them, and re-layouts  1.8 us

profile of v1, /device:TPU:1, one launch (start us, length us, event | category | flops | bytes accessed | tf_op | source)
XLA Modules:
  0.0 66.4 jit_solution(6450365249861286245)
XLA Ops:
  1.3 63.3 %shard_map.104 = (f32[2,6]{1,0:T(2,128)}, f32[1,6]{1,0:T(1,128)}) custom-call(bf16[2,16,10240]{2,1,0:T(8,128)(2,1)} %coef_ref.1, s32[3,10240]{1,0:T(4,128)} %miller_ref.1, s32[1]{0:T(128)S(6)} %copy.13.count_ref, s32[3,128]{1,0:T(4,128)} %pos_ref.1, s32[1,128]{1,0:T(1,128)} %bitcast.6, s32[1,128]{1,0:T(1,128)} %bitcast.7, f32[2,8]{1,0:T(2,128)} %radius_ref.1, ...), custom_call_target="tpu_custom_call" | custom-call | tf_op jit(solution)/shard_map/pallas_call | solution.py:258
  64.6 0.0 copy-start
  64.6 0.7 copy-done
  65.3 0.0 copy-start.1
  65.3 0.6 copy.14
  65.9 0.1 copy-done.1
  65.9 0.5 copy.15
Async XLA Ops:
  64.6 0.7 %copy-start = (f32[2,6]{1,0:T(2,128)S(1)}, f32[2,6]{1,0:T(2,128)}, u32[]{:S(2)}) copy-start(f32[2,6]{1,0:T(2,128)} %get-tuple-element.4) | copy-start | bytes 148
  65.3 0.6 copy-start.1

commit v2 on v1

--- a/solution.py
+++ b/solution.py
@@ -9,14 +9,13 @@
 from jax.sharding import PartitionSpec as P
 
 BANDS = 64
-BLOCK = 512
+BLOCK = 2560
 SIN_POLY = (4.44287957, -7.30781668, 3.59777418, -0.79119939)
 COS_POLY = (1.41420401, -6.97763732, 5.71518787, -1.72821389)
-ROUNDER = 12582912.0
 F32 = jnp.float32
 BF16 = jnp.bfloat16
-NT = (((1,), (1,)), ((), ()))
 NN = (((1,), (0,)), ((), ()))
+TN = (((0,), (0,)), ((), ()))
 
 
 def poly(coefs, y):
@@ -26,9 +25,11 @@
     return total
 
 
-def split(x):
-    high = x.astype(BF16)
-    return high, (x - high.astype(F32)).astype(BF16)
+def wheel(turns):
+    r = turns - jnp.round(turns)
+    rr = r * r
+    sine_half = poly(SIN_POLY, rr) * r
+    return 1.0 - sine_half * sine_half, sine_half * poly(COS_POLY, rr)
 
 
 def iota(shape, axis):
@@ -38,7 +39,7 @@
 def kernel(
     n_pw, n_band, coef_ref, miller_ref, count_ref, pos_ref, species_ref, slot_ref, radius_ref, strength_ref,
     occ_ref, stress_ref, kin_ref,
-    e_ref, u_ref, w_ref, acc_ref, kacc_ref, out_ref, bt_ref, zbuf, zrecv, own, gath, fbuf, frecv, bsend, brecv,
+    e_ref, t_even, t_odd, u_even, u_odd, w_ref, acc_ref, kacc_ref, out_ref, bt_ref, zbuf, zrecv, own, gath, fbuf, frecv, bsend, brecv,
     sig_ref, send_sem, recv_sem,
 ):
     columns = coef_ref.shape[2]
@@ -66,13 +67,15 @@
         for i in order:
             row = part[i : i + 1, :].astype(F32)
             place_rows.append(jnp.sum(jnp.where(one_hot, row, 0.0), axis=1, keepdims=True) * (1.0 / 4096.0))
-    place_rows += [jnp.zeros((atoms, 1), F32)] * 2
-    places = jnp.zeros((atoms, 8), F32)
-    lane8 = iota((atoms, 8), 1)
-    for i in range(6):
-        places = jnp.where(lane8 == i, place_rows[i], places)
-    places = places.astype(BF16)
     kind = jnp.sum(jnp.where(one_hot, species_ref[...].astype(F32), 0.0), axis=1, keepdims=True)
+    wide = jnp.zeros((atoms, atoms), F32)
+    wide_lane = iota((atoms, atoms), 1)
+    for i, value in enumerate(place_rows + [kind]):
+        wide = jnp.where(wide_lane == i, value, wide)
+    turned = wide.T
+    places = wide[:, 0:8].astype(BF16)
+    places_t = turned[0:8].astype(BF16)
+    kind_row = turned[6:7]
 
     row8 = iota((8, 1), 0)
     decay = []
@@ -91,28 +94,23 @@
     kacc_ref[...] = jnp.zeros_like(kacc_ref)
     count = count_ref[0]
 
-    def build(step, carry):
+    def build(step, t_ref, u_ref, slot):
         base = pl.multiple_of(step * BLOCK, BLOCK)
         cols = pl.ds(base, BLOCK)
         index = miller_ref[:, cols].astype(F32)
         x, y, z = (index[i : i + 1] for i in range(3))
         zero = jnp.zeros((2, BLOCK), F32)
         index8 = jnp.concatenate([x, y, z, y, z, x, zero], axis=0)
-        turns = lax.dot_general(places, index8.astype(BF16), NN, preferred_element_type=F32)
-        r = turns - jnp.round(turns)
-        rr = r * r
-        sine_half = poly(SIN_POLY, rr) * r
-        cosine_half = poly(COS_POLY, rr)
-        cosine = 1.0 - sine_half * sine_half
-        sine = sine_half * cosine_half
-        for half, value in enumerate((cosine, sine)):
-            high, low = split(value)
-            e_ref[0, half * atoms : (half + 1) * atoms, cols] = high
-            e_ref[1, half * atoms : (half + 1) * atoms, cols] = low
+        index_bf = index8.astype(BF16)
+        cosine, sine = wheel(lax.dot_general(places, index_bf, NN, preferred_element_type=F32))
+        e_ref[step, 0:atoms] = cosine
+        e_ref[step, atoms : 2 * atoms] = sine
+        cosine, sine = wheel(lax.dot_general(index_bf, places_t, TN, preferred_element_type=F32))
+        t_ref[:, 0:atoms] = cosine.astype(BF16)
+        t_ref[:, atoms : 2 * atoms] = sine.astype(BF16)
         weights = index8 * jnp.concatenate([x, y, z, z, x, y, zero], axis=0) * (1.0 / 64.0)
         wave_sq = weights[0:1] + weights[1:2] + weights[2:3]
-        high, low = split(weights)
-        w_ref[:, cols] = jnp.concatenate([high.astype(F32), low.astype(F32)], axis=0).astype(BF16)
+        w_ref[step] = weights
         live = (iota((1, BLOCK), 1) + base) < count
         coef = [coef_ref[ri, :, cols].astype(F32) for ri in range(2)]
         for s in range(2):
@@ -120,26 +118,38 @@
             for p in range(8):
                 row = radial[p : p + 1]
                 for ri in range(2):
-                    u_ref[pl.ds((s * 2 + ri) * atoms + p * bands, bands), cols] = (row * coef[ri]).astype(BF16)
+                    first = (s * 2 + ri) * atoms + p * bands
+                    u_ref[slot, first : first + bands] = (row * coef[ri]).astype(BF16)
         density = jnp.sum(filling * (coef[0] * coef[0] + coef[1] * coef[1]), axis=0, keepdims=True)
         moment = weights * jnp.where(live, density, 0.0)
         kacc_ref[...] += sum(moment[:, 128 * i : 128 * (i + 1)] for i in range(BLOCK // 128))
-        u = u_ref[:, cols]
-        acc_ref[...] += lax.dot_general(
-            e_ref[0, :, cols], u, NT, preferred_element_type=F32
-        ) + lax.dot_general(e_ref[1, :, cols], u, NT, preferred_element_type=F32)
+
+    def meet(t_ref, u_ref, slot):
+        acc_ref[...] += lax.dot_general(u_ref[slot], t_ref[...], NN, preferred_element_type=F32)
+
+    pairs = steps // 2
+
+    def build_pair(pair, carry):
+        build(2 * pair + 1, t_odd, u_odd, pair)
+        meet(t_even, u_even, pair)
+        build(2 * pair + 2, t_even, u_even, pair + 1)
+        meet(t_odd, u_odd, pair)
         return carry
 
-    lax.fori_loop(0, steps, build, 0)
+    build(0, t_even, u_even, 0)
+    lax.fori_loop(0, pairs - 1, build_pair, 0)
+    build(steps - 1, t_odd, u_odd, pairs - 1)
+    meet(t_even, u_even, pairs - 1)
+    meet(t_odd, u_odd, pairs - 1)
 
     rows_each = 256 // n_pw
     cross = [[], []]
     for s in range(2):
         re, im = (slice((2 * s + ri) * 128, (2 * s + ri + 1) * 128) for ri in range(2))
-        cross[0].append(acc_ref[0:128, re] - acc_ref[128:256, im])
-        cross[1].append(acc_ref[0:128, im] + acc_ref[128:256, re])
+        cross[0].append(acc_ref[re, 0:128] - acc_ref[im, 128:256])
+        cross[1].append(acc_ref[im, 0:128] + acc_ref[re, 128:256])
     for ri in range(2):
-        mixed = jnp.where(kind == 0.0, cross[ri][0], cross[ri][1])
+        mixed = jnp.where(kind_row == 0.0, cross[ri][0], cross[ri][1])
         for i in range(n_pw // 2):
             zbuf[ri * (n_pw // 2) + i] = mixed[i * rows_each : (i + 1) * rows_each]
 
@@ -186,7 +196,8 @@
         spread.append(b * fill_lane)
     settle(gath, 1, n_pw - 1)
     total = [
-        jnp.concatenate([gath[ri * (n_pw // 2) + i] for i in range(n_pw // 2)], axis=0) for ri in range(2)
+        jnp.concatenate([gath[ri * (n_pw // 2) + i] for i in range(n_pw // 2)], axis=0).T
+        for ri in range(2)
     ]
     norm = total[0] * total[0] + total[1] * total[1]
     norm = jnp.sum(norm * jnp.where(kind == 0.0, plain[0], plain[1]), axis=1, keepdims=True) * (1.0 / n_pw)
@@ -196,33 +207,31 @@
         for ri, pair in enumerate(((back_re, back_im), (back_im, -back_re))):
             lanes = slice((2 * s + ri) * 128, (2 * s + ri + 1) * 128)
             for half in range(2):
-                high, low = split(pair[0] if half == 0 else pair[1])
+                high = pair[half].astype(BF16)
                 bt_ref[half * 128 : (half + 1) * 128, lanes] = high
-                bt_ref[256 + half * 128 : 256 + (half + 1) * 128, lanes] = low
+                bt_ref[256 + half * 128 : 256 + (half + 1) * 128, lanes] = (pair[half] - high.astype(F32)).astype(BF16)
     out_ref[...] = jnp.zeros_like(out_ref)
 
-    def contract(step, carry):
-        base = pl.multiple_of(step * BLOCK, BLOCK)
-        cols = pl.ds(base, BLOCK)
-        u = u_ref[:, cols]
-        back = lax.dot_general(bt_ref[0:256], u, NN, preferred_element_type=F32) + lax.dot_general(
-            bt_ref[256:512], u, NN, preferred_element_type=F32
-        )
-        value = [e_ref[0, h * 128 : (h + 1) * 128, cols].astype(F32) for h in range(2)]
-        low = [e_ref[1, h * 128 : (h + 1) * 128, cols].astype(F32) for h in range(2)]
-        both = back[0:128] * (value[0] + low[0]) + back[128:256] * (value[1] + low[1])
-        high, low = split(both)
-        w = w_ref[:, cols]
-        out_ref[...] += lax.dot_general(high, w, NT, preferred_element_type=F32) + lax.dot_general(
-            low, w, NT, preferred_element_type=F32
-        )
+    def contract(u_ref, slot, step):
+        cols = pl.ds(pl.multiple_of(step * BLOCK, BLOCK), BLOCK)
+        back = lax.dot_general(bt_ref[...], u_ref[slot], NN, preferred_element_type=F32)
+        both = (back[0:128] + back[256:384]) * e_ref[step, 0:128] + (back[128:256] + back[384:512]) * e_ref[step, 128:256]
+        for k in range(6):
+            term = both * w_ref[step, k : k + 1]
+            out_ref[k] += sum(term[:, 128 * i : 128 * (i + 1)] for i in range(BLOCK // 128))
+
+    def contract_pair(pair, carry):
+        contract(u_even, pair, 2 * pair)
+        contract(u_odd, pair, 2 * pair + 1)
         return carry
 
-    lax.fori_loop(0, steps, contract, 0)
+    lax.fori_loop(0, pairs, contract_pair, 0)
 
     kin = jnp.sum(kacc_ref[...], axis=1, keepdims=True) * (0.5 / BANDS)
     kin_row = jnp.sum(jnp.where(iota((8, 128), 1) == iota((8, 128), 0) + 8, kin, 0.0), axis=0, keepdims=True)
-    stress = out_ref[:, 0:8] + out_ref[:, 8:16] - jnp.where(iota((1, 8), 1) < 3, norm, 0.0)
+    stress = jnp.where(iota((1, 8), 1) < 3, -norm, 0.0)
+    for k in range(6):
+        stress = stress + jnp.where(iota((1, 8), 1) == k, jnp.sum(out_ref[k], axis=1, keepdims=True), 0.0)
     sig_ref[...] = jnp.broadcast_to(kin_row, sig_ref.shape)
     sig_ref[:, 0:8] = stress
     per = atoms // n_pw
@@ -253,6 +262,7 @@
         columns = coefficients.shape[2]
         vmem = pl.BlockSpec(memory_space=pltpu.VMEM)
         smem = pl.BlockSpec(memory_space=pltpu.SMEM)
+        pairs = columns // (2 * BLOCK)
         per = 128 // n_pw
         rows = 256 // n_pw
         stress, kinetic = pl.pallas_call(
@@ -261,12 +271,15 @@
             in_specs=[vmem, vmem, smem, vmem, vmem, vmem, smem, smem, smem],
             out_specs=(vmem, vmem),
             scratch_shapes=[
-                pltpu.VMEM((2, 256, columns), BF16),
-                pltpu.VMEM((512, columns), BF16),
-                pltpu.VMEM((16, columns), BF16),
-                pltpu.VMEM((256, 512), F32),
+                pltpu.VMEM((2 * pairs, 256, BLOCK), F32),
+                pltpu.VMEM((BLOCK, 256), BF16),
+                pltpu.VMEM((BLOCK, 256), BF16),
+                pltpu.VMEM((pairs, 512, BLOCK), BF16),
+                pltpu.VMEM((pairs, 512, BLOCK), BF16),
+                pltpu.VMEM((2 * pairs, 8, BLOCK), F32),
+                pltpu.VMEM((512, 256), F32),
                 pltpu.VMEM((8, 128), F32),
-                pltpu.VMEM((128, 16), F32),
+                pltpu.VMEM((6, 128, 128), F32),
                 pltpu.VMEM((512, 512), BF16),
                 pltpu.VMEM((n_pw, rows, 128), F32),
                 pltpu.VMEM((n_pw, rows, 128), F32),

time: 66.6 us -> 56.7 us (0.85)
  Pallas kernels: 63.3 us -> 53.5 us
    pallas_call x1, Pallas kernels: 63.3 us -> 53.5 us  [on_device(): pl.pallas_call(functools.partial(kernel, n_pw, n_band), out_shape=(jax.Sh...]
where the time goes in v2:
time: 56.7 us; the launch traced here: 56.6 us
  Pallas kernels  53.5 us (94%)
  local copies, waits for them, and re-layouts  1.8 us (3%)
  between operations  1.3 us (2%)
    pallas_call x1, Pallas kernels, on_device(): pl.pallas_call(functools.partial(kernel, n_pw, n_band), out_shape=(jax.Sh...  53.5 us
    unnamed x6, local copies, waits for them, and re-layouts  1.8 us

profile of v2, /device:TPU:1, one launch (start us, length us, event | category | flops | bytes accessed | tf_op | source)
XLA Modules:
  0.0 56.6 jit_solution(13687677598321317119)
XLA Ops:
  1.3 53.5 %shard_map.104 = (f32[2,6]{1,0:T(2,128)}, f32[1,6]{1,0:T(1,128)}) custom-call(bf16[2,16,10240]{2,1,0:T(8,128)(2,1)} %coef_ref.1, s32[3,10240]{1,0:T(4,128)} %miller_ref.1, s32[1]{0:T(128)S(6)} %copy.13.count_ref, s32[3,128]{1,0:T(4,128)} %pos_ref.1, s32[1,128]{1,0:T(1,128)} %bitcast.6, s32[1,128]{1,0:T(1,128)} %bitcast.7, f32[2,8]{1,0:T(2,128)} %radius_ref.1, ...), custom_call_target="tpu_custom_call" | custom-call | tf_op jit(solution)/shard_map/pallas_call | solution.py:268
  54.8 0.0 copy-start
  54.8 0.7 %copy-done = f32[2,6]{1,0:T(2,128)S(1)} copy-done((f32[2,6]{1,0:T(2,128)S(1)}, f32[2,6]{1,0:T(2,128)}, u32[]{:S(2)}) %copy-start) | copy-done | bytes 72
  55.5 0.0 copy-start.1
  55.5 0.6 copy.14
  56.0 0.1 copy-done.1
  56.1 0.5 copy.15
Async XLA Ops:
  54.8 0.7 %copy-start = (f32[2,6]{1,0:T(2,128)S(1)}, f32[2,6]{1,0:T(2,128)}, u32[]{:S(2)}) copy-start(f32[2,6]{1,0:T(2,128)} %get-tuple-element.4) | copy-start | bytes 148
  55.5 0.6 %copy-start.1 = (f32[1,6]{1,0:T(1,128)S(1)}, f32[1,6]{1,0:T(1,128)}, u32[]{:S(2)}) copy-start(f32[1,6]{1,0:T(1,128)} %get-tuple-element.5) | copy-start | bytes 76

commit v3 on v2

--- a/solution.py
+++ b/solution.py
@@ -10,12 +10,14 @@
 
 BANDS = 64
 BLOCK = 2560
+PART = 1280
 SIN_POLY = (4.44287957, -7.30781668, 3.59777418, -0.79119939)
 COS_POLY = (1.41420401, -6.97763732, 5.71518787, -1.72821389)
 F32 = jnp.float32
 BF16 = jnp.bfloat16
 NN = (((1,), (0,)), ((), ()))
 TN = (((0,), (0,)), ((), ()))
+NT = (((1,), (1,)), ((), ()))
 
 
 def poly(coefs, y):
@@ -39,8 +41,8 @@
 def kernel(
     n_pw, n_band, coef_ref, miller_ref, count_ref, pos_ref, species_ref, slot_ref, radius_ref, strength_ref,
     occ_ref, stress_ref, kin_ref,
-    e_ref, t_even, t_odd, u_even, u_odd, w_ref, acc_ref, kacc_ref, out_ref, bt_ref, zbuf, zrecv, own, gath, fbuf, frecv, bsend, brecv,
-    sig_ref, send_sem, recv_sem,
+    t_even, t_odd, u_even, u_odd, p_even, p_odd, c_even, c_odd, acc_ref, mom_ref, tile_ref, kacc_ref, zbuf, zrecv, own, gath, fbuf,
+    frecv, bsend, brecv,     sig_ref, send_sem, recv_sem,
 ):
     columns = coef_ref.shape[2]
     bands = coef_ref.shape[1]
@@ -92,7 +94,15 @@
 
     acc_ref[...] = jnp.zeros_like(acc_ref)
     kacc_ref[...] = jnp.zeros_like(kacc_ref)
+    mom_ref[...] = jnp.zeros_like(mom_ref)
     count = count_ref[0]
+
+    def load(u_ref, s, radial, coef):
+        for p in range(8):
+            row = radial[p : p + 1]
+            for ri in range(2):
+                first = (s * 2 + ri) * atoms + p * bands
+                u_ref[first : first + bands] = (row * coef[ri]).astype(BF16)
 
     def build(step, t_ref, u_ref, slot):
         base = pl.multiple_of(step * BLOCK, BLOCK)
@@ -102,30 +112,22 @@
         zero = jnp.zeros((2, BLOCK), F32)
         index8 = jnp.concatenate([x, y, z, y, z, x, zero], axis=0)
         index_bf = index8.astype(BF16)
-        cosine, sine = wheel(lax.dot_general(places, index_bf, NN, preferred_element_type=F32))
-        e_ref[step, 0:atoms] = cosine
-        e_ref[step, atoms : 2 * atoms] = sine
         cosine, sine = wheel(lax.dot_general(index_bf, places_t, TN, preferred_element_type=F32))
         t_ref[:, 0:atoms] = cosine.astype(BF16)
         t_ref[:, atoms : 2 * atoms] = sine.astype(BF16)
         weights = index8 * jnp.concatenate([x, y, z, z, x, y, zero], axis=0) * (1.0 / 64.0)
         wave_sq = weights[0:1] + weights[1:2] + weights[2:3]
-        w_ref[step] = weights
         live = (iota((1, BLOCK), 1) + base) < count
         coef = [coef_ref[ri, :, cols].astype(F32) for ri in range(2)]
         for s in range(2):
             radial = jnp.where(live, jnp.exp(decay[s] * wave_sq), 0.0)
-            for p in range(8):
-                row = radial[p : p + 1]
-                for ri in range(2):
-                    first = (s * 2 + ri) * atoms + p * bands
-                    u_ref[slot, first : first + bands] = (row * coef[ri]).astype(BF16)
+            load(u_ref, s, radial, coef)
         density = jnp.sum(filling * (coef[0] * coef[0] + coef[1] * coef[1]), axis=0, keepdims=True)
         moment = weights * jnp.where(live, density, 0.0)
         kacc_ref[...] += sum(moment[:, 128 * i : 128 * (i + 1)] for i in range(BLOCK // 128))
 
     def meet(t_ref, u_ref, slot):
-        acc_ref[...] += lax.dot_general(u_ref[slot], t_ref[...], NN, preferred_element_type=F32)
+        acc_ref[...] += lax.dot_general(u_ref[...], t_ref[...], NN, preferred_element_type=F32)
 
     pairs = steps // 2
 
@@ -143,13 +145,16 @@
     meet(t_odd, u_odd, pairs - 1)
 
     rows_each = 256 // n_pw
-    cross = [[], []]
-    for s in range(2):
-        re, im = (slice((2 * s + ri) * 128, (2 * s + ri + 1) * 128) for ri in range(2))
-        cross[0].append(acc_ref[re, 0:128] - acc_ref[im, 128:256])
-        cross[1].append(acc_ref[im, 0:128] + acc_ref[re, 128:256])
-    for ri in range(2):
-        mixed = jnp.where(kind_row == 0.0, cross[ri][0], cross[ri][1])
+
+    def combine(ref):
+        cross = [[], []]
+        for s in range(2):
+            re, im = (slice((2 * s + ri) * 128, (2 * s + ri + 1) * 128) for ri in range(2))
+            cross[0].append(ref[re, 0:128] - ref[im, 128:256])
+            cross[1].append(ref[im, 0:128] + ref[re, 128:256])
+        return [jnp.where(kind_row == 0.0, cross[ri][0], cross[ri][1]) for ri in range(2)]
+
+    for ri, mixed in enumerate(combine(acc_ref)):
         for i in range(n_pw // 2):
             zbuf[ri * (n_pw // 2) + i] = mixed[i * rows_each : (i + 1) * rows_each]
 
@@ -171,12 +176,56 @@
         pltpu.make_async_copy(block, block, recv_sem.at[phase]).wait()
         pltpu.make_async_copy(block, block, send_sem.at[phase]).wait()
 
+    def shape(step, p_ref, c_ref):
+        base = pl.multiple_of(step * PART, PART)
+        cols = pl.ds(base, PART)
+        index = miller_ref[:, cols].astype(F32)
+        x, y, z = (index[i : i + 1] for i in range(3))
+        zero = jnp.zeros((2, PART), F32)
+        index8 = jnp.concatenate([x, y, z, y, z, x, zero], axis=0)
+        cosine, sine = wheel(lax.dot_general(places, index8.astype(BF16), NN, preferred_element_type=F32))
+        weights = index8 * jnp.concatenate([x, y, z, z, x, y, zero], axis=0) * (1.0 / 64.0)
+        wave_sq = weights[0:1] + weights[1:2] + weights[2:3]
+        for p in range(8):
+            radial = jnp.exp(fade[p] * wave_sq)
+            p_ref[p * 256 : p * 256 + 128] = (radial * cosine).astype(BF16)
+            p_ref[p * 256 + 128 : p * 256 + 256] = (radial * sine).astype(BF16)
+        live = (iota((1, PART), 1) + base) < count
+        coef = [coef_ref[ri, :, cols].astype(F32) for ri in range(2)]
+        for k in range(6):
+            row = jnp.where(live, weights[k : k + 1], 0.0)
+            for ri in range(2):
+                first = (2 * k + ri) * bands
+                c_ref[first : first + bands] = (row * coef[ri]).astype(BF16)
+
+    def meet_moments(p_ref, c_ref):
+        mom_ref[...] += lax.dot_general(p_ref[...], c_ref[...], NT, preferred_element_type=F32)
+
+    parts = columns // PART
+
+    def moments(begin, end):
+        def two(j, carry):
+            shape(2 * j + 1, p_odd, c_odd)
+            meet_moments(p_even, c_even)
+            shape(jnp.minimum(2 * j + 2, parts - 1), p_even, c_even)
+            meet_moments(p_odd, c_odd)
+            return carry
+
+        lax.fori_loop(begin, end, two, 0)
+
+    fade = []
+    for p in range(8):
+        near, far = radius_ref[0, p], radius_ref[1, p]
+        fade.append(jnp.where(kind == 0.0, -0.5 * (near * near), -0.5 * (far * far)))
     scatter(lambda to: zbuf.at[to], zrecv, 0)
+    shape(0, p_even, c_even)
+    moments(0, parts // 4)
     zrecv[me] = zbuf[me]
     settle(zrecv, 0, n_pw - 1)
     own[...] = jnp.sum(zrecv[...], axis=0)
     scatter(lambda to: own, gath, 1)
     gath[me] = own[...]
+    moments(parts // 4, parts // 2)
 
     lane = iota((1, 128), 1)
     band_lane = lax.rem(lane, bands)
@@ -194,46 +243,43 @@
             b = jnp.where(proj_lane == p, 2.0 * strength_ref[s, p] * (r * r), b)
         plain.append(a * fill_lane)
         spread.append(b * fill_lane)
+    source_row = iota((256, 12 * bands), 0)
+    target = iota((256, 12 * bands), 1)
+    same = (source_row // 128 == lax.rem(target // bands, 2)) & (lax.rem(source_row, bands) == lax.rem(target, bands))
+    for p in range(8):
+        mine = same & (lax.rem(source_row, 128) // bands == p)
+        tile_ref[p] = jnp.where(mine, 1.0, 0.0).astype(BF16)
+    plain_of = jnp.where(kind == 0.0, plain[0], plain[1])
+    spread_of = jnp.where(kind == 0.0, spread[0], spread[1])
     settle(gath, 1, n_pw - 1)
     total = [
-        jnp.concatenate([gath[ri * (n_pw // 2) + i] for i in range(n_pw // 2)], axis=0).T
-        for ri in range(2)
+        jnp.concatenate([gath[ri * (n_pw // 2) + i] for i in range(n_pw // 2)], axis=0).T for ri in range(2)
     ]
-    norm = total[0] * total[0] + total[1] * total[1]
-    norm = jnp.sum(norm * jnp.where(kind == 0.0, plain[0], plain[1]), axis=1, keepdims=True) * (1.0 / n_pw)
-    for s in range(2):
-        scale = jnp.where(kind == float(s), spread[s], 0.0)
-        back_re, back_im = total[0] * scale, total[1] * scale
-        for ri, pair in enumerate(((back_re, back_im), (back_im, -back_re))):
-            lanes = slice((2 * s + ri) * 128, (2 * s + ri + 1) * 128)
-            for half in range(2):
-                high = pair[half].astype(BF16)
-                bt_ref[half * 128 : (half + 1) * 128, lanes] = high
-                bt_ref[256 + half * 128 : 256 + (half + 1) * 128, lanes] = (pair[half] - high.astype(F32)).astype(BF16)
-    out_ref[...] = jnp.zeros_like(out_ref)
-
-    def contract(u_ref, slot, step):
-        cols = pl.ds(pl.multiple_of(step * BLOCK, BLOCK), BLOCK)
-        back = lax.dot_general(bt_ref[...], u_ref[slot], NN, preferred_element_type=F32)
-        both = (back[0:128] + back[256:384]) * e_ref[step, 0:128] + (back[128:256] + back[384:512]) * e_ref[step, 128:256]
-        for k in range(6):
-            term = both * w_ref[step, k : k + 1]
-            out_ref[k] += sum(term[:, 128 * i : 128 * (i + 1)] for i in range(BLOCK // 128))
-
-    def contract_pair(pair, carry):
-        contract(u_even, pair, 2 * pair)
-        contract(u_odd, pair, 2 * pair + 1)
-        return carry
-
-    lax.fori_loop(0, pairs, contract_pair, 0)
-
+    norm = (total[0] * total[0] + total[1] * total[1]) * plain_of
+    norm = jnp.sum(norm, axis=1, keepdims=True) * (1.0 / n_pw)
+    back = [total[0] * spread_of, total[1] * spread_of]
+    pairs_of = jnp.concatenate(
+        [jnp.concatenate([back[0], back[1]], axis=1), jnp.concatenate([back[1], -back[0]], axis=1)], axis=0
+    )
+    high = pairs_of.astype(BF16)
+    low = (pairs_of - high.astype(F32)).astype(BF16)
+    product = jnp.zeros((128, 12 * bands), F32)
+    for p in range(8):
+        tile = tile_ref[p]
+        spreadout = lax.dot_general(high, tile, NN, preferred_element_type=F32) + lax.dot_general(
+            low, tile, NN, preferred_element_type=F32
+        )
+        term = mom_ref[p * 256 : p * 256 + 256] * spreadout
+        product = product + term[0:128] + term[128:256]
+    sums = jnp.where(iota((12 * bands, 128), 0) // (2 * bands) == iota((12 * bands, 128), 1), 1.0, 0.0).astype(BF16)
+    stress = jnp.where(iota((1, 128), 1) < 3, -norm, 0.0)
+    for _ in range(3):
+        piece = product.astype(BF16)
+        stress = stress + lax.dot_general(piece, sums, NN, preferred_element_type=F32)
+        product = product - piece.astype(F32)
     kin = jnp.sum(kacc_ref[...], axis=1, keepdims=True) * (0.5 / BANDS)
     kin_row = jnp.sum(jnp.where(iota((8, 128), 1) == iota((8, 128), 0) + 8, kin, 0.0), axis=0, keepdims=True)
-    stress = jnp.where(iota((1, 8), 1) < 3, -norm, 0.0)
-    for k in range(6):
-        stress = stress + jnp.where(iota((1, 8), 1) == k, jnp.sum(out_ref[k], axis=1, keepdims=True), 0.0)
-    sig_ref[...] = jnp.broadcast_to(kin_row, sig_ref.shape)
-    sig_ref[:, 0:8] = stress
+    sig_ref[...] = stress + kin_row
     per = atoms // n_pw
     for i in range(n_pw):
         fbuf[i] = sig_ref[i * per : (i + 1) * per]
@@ -262,7 +308,7 @@
         columns = coefficients.shape[2]
         vmem = pl.BlockSpec(memory_space=pltpu.VMEM)
         smem = pl.BlockSpec(memory_space=pltpu.SMEM)
-        pairs = columns // (2 * BLOCK)
+        bands = coefficients.shape[1]
         per = 128 // n_pw
         rows = 256 // n_pw
         stress, kinetic = pl.pallas_call(
@@ -271,16 +317,18 @@
             in_specs=[vmem, vmem, smem, vmem, vmem, vmem, smem, smem, smem],
             out_specs=(vmem, vmem),
             scratch_shapes=[
-                pltpu.VMEM((2 * pairs, 256, BLOCK), F32),
                 pltpu.VMEM((BLOCK, 256), BF16),
                 pltpu.VMEM((BLOCK, 256), BF16),
-                pltpu.VMEM((pairs, 512, BLOCK), BF16),
-                pltpu.VMEM((pairs, 512, BLOCK), BF16),
-                pltpu.VMEM((2 * pairs, 8, BLOCK), F32),
+                pltpu.VMEM((512, BLOCK), BF16),
+                pltpu.VMEM((512, BLOCK), BF16),
+                pltpu.VMEM((2048, PART), BF16),
+                pltpu.VMEM((2048, PART), BF16),
+                pltpu.VMEM((12 * bands, PART), BF16),
+                pltpu.VMEM((12 * bands, PART), BF16),
                 pltpu.VMEM((512, 256), F32),
+                pltpu.VMEM((2048, 12 * bands), F32),
+                pltpu.VMEM((8, 256, 12 * bands), BF16),
                 pltpu.VMEM((8, 128), F32),
-                pltpu.VMEM((6, 128, 128), F32),
-                pltpu.VMEM((512, 512), BF16),
                 pltpu.VMEM((n_pw, rows, 128), F32),
                 pltpu.VMEM((n_pw, rows, 128), F32),
                 pltpu.VMEM((rows, 128), F32),

time: 56.7 us -> 54.4 us (0.959)
  Pallas kernels: 53.5 us -> 51.1 us
    pallas_call x1, Pallas kernels: 53.5 us -> 51.1 us  [on_device(): pl.pallas_call(functools.partial(kernel, n_pw, n_band), out_shape=(jax.Sh...]
where the time goes in v3:
time: 54.4 us; the launch traced here: 54.2 us
  Pallas kernels  51.1 us (94%)
  local copies, waits for them, and re-layouts  1.8 us (3%)
  between operations  1.3 us (2%)
    pallas_call x1, Pallas kernels, on_device(): pl.pallas_call(functools.partial(kernel, n_pw, n_band), out_shape=(jax.Sh...  51.1 us
    unnamed x6, local copies, waits for them, and re-layouts  1.8 us

profile of v3, /device:TPU:1, one launch (start us, length us, event | category | flops | bytes accessed | tf_op | source)
XLA Modules:
  0.0 54.2 jit_solution(5551497684808106245)
XLA Ops:
  1.3 51.1 %shard_map.104 = (f32[2,6]{1,0:T(2,128)}, f32[1,6]{1,0:T(1,128)}) custom-call(bf16[2,16,10240]{2,1,0:T(8,128)(2,1)} %coef_ref.1, s32[3,10240]{1,0:T(4,128)} %miller_ref.1, s32[1]{0:T(128)S(6)} %copy.13.count_ref, s32[3,128]{1,0:T(4,128)} %pos_ref.1, s32[1,128]{1,0:T(1,128)} %bitcast.6, s32[1,128]{1,0:T(1,128)} %bitcast.7, f32[2,8]{1,0:T(2,128)} %radius_ref.1, ...), custom_call_target="tpu_custom_call" | custom-call | tf_op jit(solution)/shard_map/pallas_call | solution.py:314
  52.4 0.0 copy-start
  52.4 0.7 %copy-done = f32[2,6]{1,0:T(2,128)S(1)} copy-done((f32[2,6]{1,0:T(2,128)S(1)}, f32[2,6]{1,0:T(2,128)}, u32[]{:S(2)}) %copy-start) | copy-done | bytes 72
  53.1 0.0 copy-start.1
  53.1 0.6 %copy.14 = f32[6,2]{0,1:T(2,128)} copy(f32[6,2]{0,1:T(2,128)S(1)} %bitcast.5) | data formatting | bytes 96
  53.7 0.1 copy-done.1
  53.7 0.5 copy.15
Async XLA Ops:
  52.4 0.7 %copy-start = (f32[2,6]{1,0:T(2,128)S(1)}, f32[2,6]{1,0:T(2,128)}, u32[]{:S(2)}) copy-start(f32[2,6]{1,0:T(2,128)} %get-tuple-element.4) | copy-start | bytes 148
  53.1 0.6 %copy-start.1 = (f32[1,6]{1,0:T(1,128)S(1)}, f32[1,6]{1,0:T(1,128)}, u32[]{:S(2)}) copy-start(f32[1,6]{1,0:T(1,128)} %get-tuple-element.5) | copy-start | bytes 76
